TPU v7x, 32 devices: a whole 2x2x4 slice. The times are simulated.
32 devices in a mesh: groups: 2 (over x), ctx: 8 (over z, y), head: 2 (over core).
Axes of the slice: x: 2, y: 2, z: 4, core: 2. Of those that a mesh axis runs over, the one named last changes fastest.
Arguments:
- queries: bfloat16 [4096, 2048], P(('groups', 'ctx'), 'head'), parts along dimension 0, may hold values from -12 to 12
- span_keys: bfloat16 [4096, 2048], P(('groups', 'ctx'), 'head'), parts along dimension 0, may hold values from -12 to 12
- span_values: bfloat16 [4096, 2048], P(('groups', 'ctx'), 'head'), parts along dimension 0, may hold values from -6 to 6
- cache_keys: bfloat16 [8192, 2048], P(('groups', 'ctx'), 'head'), parts along dimension 0, may hold values from -12 to 12
- cache_values: bfloat16 [8192, 2048], P(('groups', 'ctx'), 'head'), parts along dimension 0, may hold values from -6 to 6
- routes: int32 [2, 32, 8, 4], P('head', ('groups', 'ctx')), parts along dimension 1, may hold values from 0 to 7, all different within a row; in each aligned block of 16 rows (0 to 15, 16 to 31, ..., all dimensions but the last counted through in order) at most 16 rows name the same one
- out_weight: bfloat16 [2048, 4096], P('head'), may hold values from -0.125 to 0.125
Outputs:
- projected: bfloat16 [4096, 4096], P(('groups', 'ctx'), 'head'), parts along dimension 0
There are 2 independent parts, one for each index of `groups`. A program takes and returns all parts, laid end to end along the dimension named above; an argument that names none is the same for every part. Nothing has to cross between parts.
Inputs may be any that keep to these rules, and one draw needn't show every extreme that they name: `routes`: each row names 4 different key blocks; among the 16 rows of one device no key block is named more than 16 times.
All inputs are finite; a program needn't handle non-finite values.
Results may differ from a plain program's by a relative error of at most 0.0064.
Values may be sent and summed in bfloat16 or wider, within the bound.
A program may use at most 128 MiB of HBM per device.

v0:
```python
import math
import jax
import jax.numpy as jnp
from jax import lax
from jax.sharding import PartitionSpec as P

DH = 128
QB = 128


def shortened(value):

    def short(part):
        return part.astype(jnp.bfloat16) if part.dtype == jnp.float32 else part

    return jax.tree.map(short, value)


def soft_partial(scores, values_block, pattern):
    highest = jnp.max(scores, axis=-1, keepdims=True)
    exponent = jnp.exp(scores - highest)
    denominator = jnp.sum(exponent, axis=-1, keepdims=True)
    weights_low = (exponent / denominator).astype(jnp.bfloat16)
    result = jnp.einsum(
        pattern, weights_low, values_block, preferred_element_type=jnp.float32
    ).astype(jnp.bfloat16)
    log_total = highest[..., 0] + jnp.log(denominator[..., 0])
    return (result, log_total)


def on_device(queries, span_keys, span_values, cache_keys, cache_values, routes, out_weight):
    blocks = routes.shape[1]
    heads_here = routes.shape[2]
    top_picks = routes.shape[3]
    key_rows = cache_keys.shape[0]
    devices = lax.axis_size("ctx")
    scaling = 1.0 / math.sqrt(DH)
    blocked = queries.reshape(blocks, QB, heads_here, DH)
    most_rows = max(2, 2 * blocks * heads_here * top_picks // devices)
    groups = 1
    per_peer = groups * most_rows
    slot_total = per_peer * devices
    wanted = routes.reshape(-1)
    item_count = wanted.shape[0]
    item_ids = jnp.arange(item_count, dtype=jnp.int32)
    block_of = item_ids // (heads_here * top_picks)
    head_of = item_ids // top_picks % heads_here
    bucket = wanted * groups + block_of % groups
    one_hot = (bucket[:, None] == jnp.arange(devices * groups, dtype=jnp.int32)[None, :]).astype(
        jnp.int32
    )
    ranking = jnp.sum(jnp.cumsum(one_hot, axis=0) * one_hot, axis=1) - 1
    position = (block_of % groups * most_rows + ranking) * devices + wanted
    matches = position[None, :] == jnp.arange(slot_total, dtype=jnp.int32)[:, None]
    filled = jnp.any(matches, axis=1)
    source = jnp.sum(jnp.where(matches, item_ids[None, :], 0), axis=1)
    gathered = blocked[block_of[source], :, head_of[source], :]
    slot_queries = jnp.where(filled[:, None, None], gathered, jnp.zeros_like(gathered)).reshape(
        per_peer, devices, QB, DH
    )
    slot_heads = jnp.where(filled, head_of[source], 0).reshape(per_peer, devices)
    keys_by_head = cache_keys.reshape(key_rows, heads_here, DH).transpose(1, 0, 2)
    values_by_head = cache_values.reshape(key_rows, heads_here, DH).transpose(1, 0, 2)

    def one_portion(portion):
        queried, head_ids = portion
        chosen_keys = keys_by_head[head_ids]
        chosen_values = values_by_head[head_ids]
        scores = (
            jnp.einsum("pqd,pkd->pqk", queried, chosen_keys, preferred_element_type=jnp.float32)
            * scaling
        )
        return soft_partial(scores, chosen_values, "pqk,pkd->pqd")

    outputs, log_sums = lax.map(
        one_portion,
        (
            lax.all_to_all(slot_queries, "ctx", split_axis=1, concat_axis=1, tiled=True),
            lax.all_to_all(slot_heads, "ctx", split_axis=1, concat_axis=1, tiled=True),
        ),
    )
    outputs_back = jax.tree.map(
        lambda part, own: part.astype(own.dtype),
        lax.all_to_all(shortened(outputs), "ctx", split_axis=1, concat_axis=1, tiled=True),
        outputs,
    )
    sums_back = lax.all_to_all(log_sums, "ctx", split_axis=1, concat_axis=1, tiled=True)
    routed_out = outputs_back.reshape(slot_total, QB, DH)[position].reshape(
        blocks, heads_here, top_picks, QB, DH
    )
    routed_lse = sums_back.reshape(slot_total, QB)[position].reshape(
        blocks, heads_here, top_picks, QB
    )
    own_keys = span_keys.reshape(blocks, QB, heads_here, DH)
    own_values = span_values.reshape(blocks, QB, heads_here, DH)
    causal = jnp.arange(QB)[:, None] >= jnp.arange(QB)[None, :]
    self_scores = (
        jnp.einsum("bqhd,bkhd->bhqk", blocked, own_keys, preferred_element_type=jnp.float32)
        * scaling
    )
    self_scores = jnp.where(causal[None, None], self_scores, -jnp.inf)
    self_out, self_lse = soft_partial(self_scores, own_values, "bhqk,bkhd->bhqd")
    all_lse = jnp.concatenate([routed_lse, self_lse[:, :, None]], axis=2)
    all_out = jnp.concatenate(
        [routed_out.astype(jnp.float32), self_out[:, :, None].astype(jnp.float32)], axis=2
    )
    highest = jnp.max(all_lse, axis=2, keepdims=True)
    merge_weights = jnp.exp(all_lse - highest)
    merge_weights = merge_weights / jnp.sum(merge_weights, axis=2, keepdims=True)
    attention = jnp.sum(merge_weights[..., None] * all_out, axis=2)
    attention = (
        attention.transpose(0, 2, 1, 3).reshape(blocks * QB, heads_here * DH).astype(jnp.bfloat16)
    )
    partial_sums = jnp.dot(attention, out_weight, preferred_element_type=jnp.float32)
    return lax.psum_scatter(partial_sums, "head", scatter_dimension=1, tiled=True).astype(
        jnp.bfloat16
    )


def solution(mesh):
    placed = (
        P(("groups", "ctx"), "head"),
        P(("groups", "ctx"), "head"),
        P(("groups", "ctx"), "head"),
        P(("groups", "ctx"), "head"),
        P(("groups", "ctx"), "head"),
        P("head", ("groups", "ctx"), None, None),
        P("head", None),
    )
    return jax.shard_map(
        on_device,
        mesh=mesh,
        in_specs=placed,
        out_specs=P(("groups", "ctx"), "head"),
        check_vma=False,
    )
```

profile of v0, /device:TPU:0, one launch (start us, length us, event | category | flops | bytes accessed | tf_op | source)
XLA Modules:
  0.0 391.5 jit_solution(3078422564545863952)
XLA Ops:
  10.0 7.3 %all-to-all-start.1 = ((s32[16,8,1]{0,2,1:T(1,128)}), s32[16,8,1]{0,2,1:T(1,128)S(1)}, u32[]{:S(2)}, u32[]{:S(2)}) async-start(s32[16,8,1]{0,2,1:T(1,128)} %copy.97), calls=%async_computation.1 | async-start | bytes 8192 | tf_op jit(solution)/shard_map/all_to_all | solution.py:79
  20.8 3.1 gather_fusion.4
  23.8 3.8 copy_select_fusion
  27.6 6.1 %all-to-all-start = ((bf16[16,8,128,128]{3,2,0,1:T(8,128)(2,1)}), bf16[16,8,128,128]{3,2,0,1:T(8,128)(2,1)}, u32[]{:S(2)}, u32[]{:S(2)}) async-start(bf16[16,8,128,128]{3,2,0,1:T(8,128)(2,1)} %copy_select_fusion), calls=%async_computation | async-start | bytes 8388608 | tf_op jit(solution)/shard_map/all_to_all | solution.py:78
  37.6 88.9 %all-to-all-done = bf16[16,8,128,128]{3,2,0,1:T(8,128)(2,1)} async-done(((bf16[16,8,128,128]{3,2,0,1:T(8,128)(2,1)}), bf16[16,8,128,128]{3,2,0,1:T(8,128)(2,1)}, u32[]{:S(2)}, u32[]{:S(2)}) %all-to-all-start) | async-done | bytes 4194336 | tf_op jit(solution)/shard_map/all_to_all | solution.py:78
  126.5 119.4 %while.13 = (s32[]{:T(128)}, bf16[16,8,128,128]{3,2,0,1:T(8,128)(2,1)}, f32[16,8,128]{2,0,1:T(8,128)S(1)}, bf16[16,8,128,128]{3,2,0,1:T(8,128)(2,1)}, s32[16,8]{...) while((s32[]{:T(128)}, bf16[16,8,128,128]{3,2,0,1:T(8,128)(2,1)}, ...), condition=%wide.region_7.8_spmd.clone, body=%wide.region_4.7_spmd.sunk.clone | while | flops 273285152 | bytes 13153525 | solution.py:75
  126.5 2.0 gather_fusion.1
  130.5 2.0 gather_fusion
  133.9 2.0 gather_fusion.1
  138.0 2.0 gather_fusion
  141.4 2.0 gather_fusion.1
  145.4 2.0 gather_fusion
  148.8 2.0 gather_fusion.1
  152.9 2.0 gather_fusion
  156.3 2.0 gather_fusion.1
  160.3 2.0 gather_fusion
  163.8 2.0 gather_fusion.1
  165.7 1.5 multiply_reduce_fusion.4
  167.8 2.0 gather_fusion
  171.2 2.0 gather_fusion.1
  175.3 2.0 gather_fusion
  178.7 2.0 gather_fusion.1
  182.7 2.0 gather_fusion
  186.1 2.0 gather_fusion.1
  190.2 2.0 gather_fusion
  193.6 2.0 gather_fusion.1
  197.6 2.0 gather_fusion
  201.1 2.0 gather_fusion.1
  205.1 2.0 gather_fusion
  208.5 2.0 gather_fusion.1
  212.6 2.0 gather_fusion
  216.0 2.0 gather_fusion.1
  220.0 2.0 gather_fusion
  223.5 2.0 gather_fusion.1
  227.5 2.0 gather_fusion
  230.9 2.0 gather_fusion.1
  235.0 2.0 gather_fusion
  238.4 2.0 gather_fusion.1
  242.5 2.0 gather_fusion
  245.8 10.3 %all_to_all.24 = f32[16,8,128]{2,0,1:T(8,128)S(1)} all-to-all(f32[16,8,128]{2,0,1:T(8,128)S(1)} %get-tuple-element.43), channel_id=1, replica_groups=mesh['groups'=2,'ctx'=8,'head'=2] {'ctx'}, dimensions={1} | all-to-all | bytes 131072 | tf_op jit(solution)/shard_map/all_to_all | solution.py:87
  256.2 4.7 %all-to-all-start.3 = ((bf16[16,8,128,128]{3,2,0,1:T(8,128)(2,1)}), bf16[16,8,128,128]{3,2,0,1:T(8,128)(2,1)}, u32[]{:S(2)}, u32[]{:S(2)}) async-start(bf16[16,8,128,128]{3,2,0,1:T(8,128)(2,1)} %get-tuple-element.44), calls=%async_computation.3 | async-start | bytes 8388608 | tf_op jit(solution)/shard_map/all_to_all | solution.py:84
  263.7 89.5 %all-to-all-done.3 = bf16[16,8,128,128]{3,2,0,1:T(8,128)(2,1)} async-done(((bf16[16,8,128,128]{3,2,0,1:T(8,128)(2,1)}), bf16[16,8,128,128]{3,2,0,1:T(8,128)(2,1)}, u32[]{:S(2)}, u32[]{:S(2)}) %all-to-all-start.3) | async-done | bytes 4194336 | tf_op jit(solution)/shard_map/all_to_all | solution.py:84
  353.2 4.7 %copy.112 = bf16[16,8,128,128]{3,2,1,0:T(8,128)(2,1)} copy(bf16[16,8,128,128]{3,2,0,1:T(8,128)(2,1)} %all-to-all-done.3) | data formatting | bytes 8388608 | tf_op jit(solution)/shard_map/all_to_all | solution.py:84
  357.9 3.1 gather_fusion.6
  361.1 1.8 multiply_reduce_fusion.1
  363.2 7.6 %fusion.15 = f32[256,4096]{1,0:T(8,128)} fusion(bf16[1024,4096]{1,0:T(8,128)(2,1)} %param.15, bf16[32,8,8,128]{3,2,1,0:T(8,128)(2,1)S(1)} %bitcast.116), kind=kOutput, calls=%fused_computation.36 | convolution fusion | flops 2147483648 | bytes 13107200 | tf_op jit(solution)/shard_map/dot_general | solution.py:114
  370.9 11.1 %reduce-scatter.2.cloned.1.call-done = f32[256,2048]{1,0:T(8,128)} async-done(((f32[256,4096]{1,0:T(8,128)}), f32[256,2048]{1,0:T(8,128)}) %reduce-scatter.2.cloned.1.call-update) | async-done | bytes 2097168 | tf_op jit(solution)/shard_map/reduce_scatter | solution.py:115
  382.0 2.7 convert_element_type.43
  (170 shorter events, 67.5 us)
Async XLA Ops:
  10.0 17.6 %all-to-all-start.1 = ((s32[16,8,1]{0,2,1:T(1,128)}), s32[16,8,1]{0,2,1:T(1,128)S(1)}, u32[]{:S(2)}, u32[]{:S(2)}) async-start(s32[16,8,1]{0,2,1:T(1,128)} %copy.97), calls=%async_computation.1 | async-start | bytes 8192 | tf_op jit(solution)/shard_map/all_to_all | solution.py:79
  19.8 0.8 copy-start
  27.6 6.2 %copy-start.2 = (bf16[512,1024]{1,0:T(8,128)(2,1)S(1)}, bf16[512,1024]{1,0:T(8,128)(2,1)}, u32[]{:S(2)}) copy-start(bf16[512,1024]{1,0:T(8,128)(2,1)} %param.12) | copy-start | bytes 3145732
  27.6 98.9 %all-to-all-start = ((bf16[16,8,128,128]{3,2,0,1:T(8,128)(2,1)}), bf16[16,8,128,128]{3,2,0,1:T(8,128)(2,1)}, u32[]{:S(2)}, u32[]{:S(2)}) async-start(bf16[16,8,128,128]{3,2,0,1:T(8,128)(2,1)} %copy_select_fusion), calls=%async_computation | async-start | bytes 8388608 | tf_op jit(solution)/shard_map/all_to_all | solution.py:78
  33.7 1.9 copy-start.3
  256.2 4.8 %copy-start.4 = (bf16[256,1024]{1,0:T(8,128)(2,1)S(1)}, bf16[256,1024]{1,0:T(8,128)(2,1)}, u32[]{:S(2)}) copy-start(bf16[256,1024]{1,0:T(8,128)(2,1)} %param.10) | copy-start | bytes 1572868
  256.2 4.9 %copy-start.5 = (bf16[256,1024]{1,0:T(8,128)(2,1)S(1)}, bf16[256,1024]{1,0:T(8,128)(2,1)}, u32[]{:S(2)}) copy-start(bf16[256,1024]{1,0:T(8,128)(2,1)} %param.11) | copy-start | bytes 1572868
  256.2 5.1 %copy-start.1 = (bf16[32,8,8,128]{3,2,1,0:T(8,128)(2,1)S(1)}, bf16[32,8,8,128]{3,2,1,0:T(8,128)(2,1)}, u32[]{:S(2)}) copy-start(bf16[32,8,8,128]{3,2,1,0:T(8,128)(2,1)} %copy-done) | copy-start | bytes 1572868
  256.2 97.0 %all-to-all-start.3 = ((bf16[16,8,128,128]{3,2,0,1:T(8,128)(2,1)}), bf16[16,8,128,128]{3,2,0,1:T(8,128)(2,1)}, u32[]{:S(2)}, u32[]{:S(2)}) async-start(bf16[16,8,128,128]{3,2,0,1:T(8,128)(2,1)} %get-tuple-element.44), calls=%async_computation.3 | async-start | bytes 8388608 | tf_op jit(solution)/shard_map/all_to_all | solution.py:84
  260.9 121.1 %reduce-scatter.2.cloned.1.call-start = ((), (), s32[]{:S(2)}) async-start(), calls=%async_computation.5 | async-start | bytes 6291456 | tf_op jit(solution)/shard_map/reduce_scatter | solution.py:115
Sparse Core Ops, SparseCore 0:
  371.0 10.9 reduce-scatter.1
where the time goes:
time: 394 us; the launch traced here: 392 us
  waiting for transfers between devices  189 us (48%)
  local copies, waits for them, and re-layouts  85.9 us (22%)
  matrix products  53.8 us (14%)
  other arithmetic  19.3 us (5%)
  starting transfers between devices  18.2 us (5%)
  between operations  13.7 us (3%)
  blocking collectives  10.3 us (3%)
    all_to_all x1, waiting for transfers between devices, on_device(): lax.all_to_all(shortened(outputs), 'ctx', split_axis=1, concat_axis=1, ti...  89.5 us
    all_to_all x1, waiting for transfers between devices, on_device(): lax.all_to_all(slot_queries, 'ctx', split_axis=1, concat_axis=1, tiled=True)  88.9 us
    gather x16, local copies, waits for them, and re-layouts, one_portion(): chosen_keys = keys_by_head[head_ids]  31.6 us
    gather x16, local copies, waits for them, and re-layouts, one_portion(): chosen_values = values_by_head[head_ids]  31.6 us
    dot_general x16, matrix products, one_portion(): jnp.einsum('pqd,pkd->pqk', queried, chosen_keys, preferred_element_type=j...  23.6 us
    dot_general x17, matrix products, soft_partial(): jnp.einsum(pattern, weights_low, values_block, preferred_element_type=jnp...  22.1 us
    reduce_scatter x1, waiting for transfers between devices, on_device(): lax.psum_scatter(partial_sums, 'head', scatter_dimension=1, tiled=True)  11.1 us
    all_to_all x1, blocking collectives, on_device(): lax.all_to_all(log_sums, 'ctx', split_axis=1, concat_axis=1, tiled=True)  10.3 us
  transfers between devices with their start and end apart: 4, of which 3 were waited for; matrix products, arithmetic and copies ran while one was open for 4% of the time, Pallas kernels for 0%

commit v1 on v0

--- a/solution.py
+++ b/solution.py
@@ -3,9 +3,17 @@
 import jax.numpy as jnp
 from jax import lax
 from jax.sharding import PartitionSpec as P
+from jax.lax import all_to_all, axis_size
 
 DH = 128
 QB = 128
+
+
+def follow_words(patch, array_dim, where_dim=1):
+    return jnp.concatenate(
+        all_to_all(jnp.stack(jnp.split(patch, axis_size("ctx"), axis=array_dim)), "ctx", 0, 0),
+        axis=where_dim,
+    )
 
 
 def shortened(value):
@@ -75,7 +83,7 @@
     outputs, log_sums = lax.map(
         one_portion,
         (
-            lax.all_to_all(slot_queries, "ctx", split_axis=1, concat_axis=1, tiled=True),
+            follow_words(slot_queries, 1),
             lax.all_to_all(slot_heads, "ctx", split_axis=1, concat_axis=1, tiled=True),
         ),
     )

time: 394 us -> 399 us (1.013)
  local copies, waits for them, and re-layouts: 85.9 us -> 92.6 us
    unnamed x18 -> x25, local copies, waits for them, and re-layouts: 3.96 us -> 9.98 us
  transfers between devices with their start and end apart: 4 -> 4, of which waited for: 3 -> 3; matrix products, arithmetic and copies ran while one was open for 4% -> 5% of each run, Pallas kernels for 0% -> 0%
where the time goes in v1:
time: 399 us; the launch traced here: 397 us
  waiting for transfers between devices  189 us (47%)
  local copies, waits for them, and re-layouts  92.6 us (23%)
  matrix products  53.8 us (13%)
  starting transfers between devices  18.2 us (5%)
  other arithmetic  18.1 us (5%)
  between operations  13.7 us (3%)
  blocking collectives  10.3 us (3%)
    all_to_all x1, waiting for transfers between devices, on_device(): lax.all_to_all(shortened(outputs), 'ctx', split_axis=1, concat_axis=1, ti...  89.5 us
    all_to_all x1, waiting for transfers between devices, follow_words(): all_to_all(jnp.stack(jnp.split(patch, axis_size('ctx'), axis=array_dim)),...  88.9 us
    gather x16, local copies, waits for them, and re-layouts, one_portion(): chosen_keys = keys_by_head[head_ids]  31.6 us
    gather x16, local copies, waits for them, and re-layouts, one_portion(): chosen_values = values_by_head[head_ids]  31.6 us
    dot_general x16, matrix products, one_portion(): jnp.einsum('pqd,pkd->pqk', queried, chosen_keys, preferred_element_type=j...  23.6 us
    dot_general x17, matrix products, soft_partial(): jnp.einsum(pattern, weights_low, values_block, preferred_element_type=jnp...  22.1 us
    reduce_scatter x1, waiting for transfers between devices, on_device(): lax.psum_scatter(partial_sums, 'head', scatter_dimension=1, tiled=True)  11.1 us
    all_to_all x1, blocking collectives, on_device(): lax.all_to_all(log_sums, 'ctx', split_axis=1, concat_axis=1, tiled=True)  10.3 us
  transfers between devices with their start and end apart: 4, of which 3 were waited for; matrix products, arithmetic and copies ran while one was open for 5% of the time, Pallas kernels for 0%

profile of v1, /device:TPU:0, one launch (start us, length us, event | category | flops | bytes accessed | tf_op | source)
XLA Modules:
  0.0 397.1 jit_solution(585826026625413593)
XLA Ops:
  10.0 7.3 %all-to-all-start.1 = ((s32[16,8,1]{0,2,1:T(1,128)}), s32[16,8,1]{0,2,1:T(1,128)S(1)}, u32[]{:S(2)}, u32[]{:S(2)}) async-start(s32[16,8,1]{0,2,1:T(1,128)} %copy.135), calls=%async_computation.1 | async-start | bytes 8192 | tf_op jit(solution)/shard_map/all_to_all | solution.py:87
  20.7 3.1 gather_fusion.4
  23.7 2.5 broadcast_select_fusion
  33.2 6.1 %all-to-all-start = ((bf16[8,16,1,128,128]{4,3,1,2,0:T(8,128)(2,1)}), bf16[8,16,1,128,128]{4,3,1,2,0:T(8,128)(2,1)}, u32[]{:S(2)}, u32[]{:S(2)}) async-start(bf16[8,16,1,128,128]{4,3,1,2,0:T(8,128)(2,1)} %fusion.18), calls=%async_computation | async-start | bytes 8388608 | tf_op jit(solution)/shard_map/all_to_all | solution.py:14
  43.2 88.9 %all-to-all-done = bf16[8,16,1,128,128]{4,3,1,2,0:T(8,128)(2,1)} async-done(((bf16[8,16,1,128,128]{4,3,1,2,0:T(8,128)(2,1)}), bf16[8,16,1,128,128]{4,3,1,2,0:T(8,128)(2,1)}, u32[]{:S(2)}, u32[]{:S(2)}) %all-to-all-start) | async-done | bytes 4194336 | tf_op jit(solution)/shard_map/all_to_all | solution.py:14
  132.0 119.4 %while.12 = (s32[]{:T(128)}, bf16[16,8,128,128]{3,2,0,1:T(8,128)(2,1)}, f32[16,8,128]{2,0,1:T(8,128)S(1)}, bf16[16,8,128,128]{3,2,0,1:T(8,128)(2,1)}, s32[16,8]{...) while((s32[]{:T(128)}, ...), condition=%wide.region_7.8_spmd, body=%wide.region_4.7_spmd.sunk | while | flops 273285152 | bytes 13153541 | solution.py:83
  132.0 2.0 gather_fusion.1
  136.1 2.0 gather_fusion
  139.5 2.0 gather_fusion.1
  143.5 2.0 gather_fusion
  146.9 2.0 gather_fusion.1
  151.0 2.0 gather_fusion
  154.4 2.0 gather_fusion.1
  158.4 2.0 gather_fusion
  161.9 2.0 gather_fusion.1
  165.9 2.0 gather_fusion
  169.3 2.0 gather_fusion.1
  171.3 1.5 multiply_reduce_fusion.3
  173.4 2.0 gather_fusion
  176.8 2.0 gather_fusion.1
  180.8 2.0 gather_fusion
  184.2 2.0 gather_fusion.1
  188.3 2.0 gather_fusion
  191.7 2.0 gather_fusion.1
  195.7 2.0 gather_fusion
  199.2 2.0 gather_fusion.1
  203.2 2.0 gather_fusion
  206.6 2.0 gather_fusion.1
  210.7 2.0 gather_fusion
  214.1 2.0 gather_fusion.1
  218.1 2.0 gather_fusion
  221.6 2.0 gather_fusion.1
  225.6 2.0 gather_fusion
  229.0 2.0 gather_fusion.1
  233.1 2.0 gather_fusion
  236.5 2.0 gather_fusion.1
  240.5 2.0 gather_fusion
  244.0 2.0 gather_fusion.1
  248.0 2.0 gather_fusion
  251.4 10.3 %all_to_all.24 = f32[16,8,128]{2,0,1:T(8,128)S(1)} all-to-all(f32[16,8,128]{2,0,1:T(8,128)S(1)} %get-tuple-element.43), channel_id=1, replica_groups=mesh['groups'=2,'ctx'=8,'head'=2] {'ctx'}, dimensions={1} | all-to-all | bytes 131072 | tf_op jit(solution)/shard_map/all_to_all | solution.py:95
  261.7 4.7 %all-to-all-start.3 = ((bf16[16,8,128,128]{3,2,0,1:T(8,128)(2,1)}), bf16[16,8,128,128]{3,2,0,1:T(8,128)(2,1)}, u32[]{:S(2)}, u32[]{:S(2)}) async-start(bf16[16,8,128,128]{3,2,0,1:T(8,128)(2,1)} %get-tuple-element.44), calls=%async_computation.3 | async-start | bytes 8388608 | tf_op jit(solution)/shard_map/all_to_all | solution.py:92
  269.2 89.5 %all-to-all-done.3 = bf16[16,8,128,128]{3,2,0,1:T(8,128)(2,1)} async-done(((bf16[16,8,128,128]{3,2,0,1:T(8,128)(2,1)}), bf16[16,8,128,128]{3,2,0,1:T(8,128)(2,1)}, u32[]{:S(2)}, u32[]{:S(2)}) %all-to-all-start.3) | async-done | bytes 4194336 | tf_op jit(solution)/shard_map/all_to_all | solution.py:92
  358.7 4.7 %copy.149 = bf16[16,8,128,128]{3,2,1,0:T(8,128)(2,1)} copy(bf16[16,8,128,128]{3,2,0,1:T(8,128)(2,1)} %all-to-all-done.3) | data formatting | bytes 8388608 | tf_op jit(solution)/shard_map/all_to_all | solution.py:92
  363.5 3.1 gather_fusion.6
  366.6 1.8 multiply_reduce_fusion.1
  368.8 7.6 %fusion.15 = f32[256,4096]{1,0:T(8,128)} fusion(bf16[1024,4096]{1,0:T(8,128)(2,1)} %param.15, bf16[32,8,8,128]{3,2,1,0:T(8,128)(2,1)S(1)} %bitcast.158), kind=kOutput, calls=%fused_computation.36 | convolution fusion | flops 2147483648 | bytes 13107200 | tf_op jit(solution)/shard_map/dot_general | solution.py:122
  376.4 11.1 %reduce-scatter.2.cloned.1.call-done = f32[256,2048]{1,0:T(8,128)} async-done(((f32[256,4096]{1,0:T(8,128)}), f32[256,2048]{1,0:T(8,128)}) %reduce-scatter.2.cloned.1.call-update) | async-done | bytes 2097168 | tf_op jit(solution)/shard_map/reduce_scatter | solution.py:123
  387.5 2.7 convert_element_type.43
  (177 shorter events, 74.3 us)
Async XLA Ops:
  10.0 23.2 %all-to-all-start.1 = ((s32[16,8,1]{0,2,1:T(1,128)}), s32[16,8,1]{0,2,1:T(1,128)S(1)}, u32[]{:S(2)}, u32[]{:S(2)}) async-start(s32[16,8,1]{0,2,1:T(1,128)} %copy.135), calls=%async_computation.1 | async-start | bytes 8192 | tf_op jit(solution)/shard_map/all_to_all | solution.py:87
  19.8 0.8 copy-start
  33.1 6.2 %copy-start.2 = (bf16[512,1024]{1,0:T(8,128)(2,1)S(1)}, bf16[512,1024]{1,0:T(8,128)(2,1)}, u32[]{:S(2)}) copy-start(bf16[512,1024]{1,0:T(8,128)(2,1)} %param.12) | copy-start | bytes 3145732
  33.2 98.9 %all-to-all-start = ((bf16[8,16,1,128,128]{4,3,1,2,0:T(8,128)(2,1)}), bf16[8,16,1,128,128]{4,3,1,2,0:T(8,128)(2,1)}, u32[]{:S(2)}, u32[]{:S(2)}) async-start(bf16[8,16,1,128,128]{4,3,1,2,0:T(8,128)(2,1)} %fusion.18), calls=%async_computation | async-start | bytes 8388608 | tf_op jit(solution)/shard_map/all_to_all | solution.py:14
  39.3 1.9 copy-start.3
  261.7 4.8 %copy-start.4 = (bf16[256,1024]{1,0:T(8,128)(2,1)S(1)}, bf16[256,1024]{1,0:T(8,128)(2,1)}, u32[]{:S(2)}) copy-start(bf16[256,1024]{1,0:T(8,128)(2,1)} %param.10) | copy-start | bytes 1572868
  261.7 4.9 %copy-start.5 = (bf16[256,1024]{1,0:T(8,128)(2,1)S(1)}, bf16[256,1024]{1,0:T(8,128)(2,1)}, u32[]{:S(2)}) copy-start(bf16[256,1024]{1,0:T(8,128)(2,1)} %param.11) | copy-start | bytes 1572868
  261.7 5.1 %copy-start.1 = (bf16[32,8,8,128]{3,2,1,0:T(8,128)(2,1)S(1)}, bf16[32,8,8,128]{3,2,1,0:T(8,128)(2,1)}, u32[]{:S(2)}) copy-start(bf16[32,8,8,128]{3,2,1,0:T(8,128)(2,1)} %copy-done) | copy-start | bytes 1572868
  261.7 97.0 %all-to-all-start.3 = ((bf16[16,8,128,128]{3,2,0,1:T(8,128)(2,1)}), bf16[16,8,128,128]{3,2,0,1:T(8,128)(2,1)}, u32[]{:S(2)}, u32[]{:S(2)}) async-start(bf16[16,8,128,128]{3,2,0,1:T(8,128)(2,1)} %get-tuple-element.44), calls=%async_computation.3 | async-start | bytes 8388608 | tf_op jit(solution)/shard_map/all_to_all | solution.py:92
  266.4 121.1 %reduce-scatter.2.cloned.1.call-start = ((), (), s32[]{:S(2)}) async-start(), calls=%async_computation.5 | async-start | bytes 6291456 | tf_op jit(solution)/shard_map/reduce_scatter | solution.py:123
Sparse Core Ops, SparseCore 0:
  376.6 10.9 reduce-scatter.1
